TPU v7x, 32 devices: a whole 2x2x4 slice. The times are simulated.
32 devices in a mesh: row: 4 (over x, core), col: 8 (over z, y).
Axes of the slice: x: 2, y: 2, z: 4, core: 2. Of those that a mesh axis runs over, the one named last changes fastest.
Arguments:
- hidden_in: bfloat16 [4, 8, 512, 896], P('row', 'col'), may hold values from -6 to 6
- targets: bfloat16 [4, 8, 512, 896], P('row', 'col'), may hold values from -6 to 6
- first_params: float32 [4, 896, 896], P('row', 'col'), may hold values from -0.1875 to 0.1875
- first_moment: float32 [4, 896, 896], P('row', 'col'), may hold values from -0.06 to 0.06
- second_params: float32 [8, 896, 896], P('col', 'row'), may hold values from -0.1875 to 0.1875
- second_moment: float32 [8, 896, 896], P('col', 'row'), may hold values from -0.06 to 0.06
Outputs:
- first_params_new: float32 [4, 896, 896], P('row', 'col')
- first_moment_new: float32 [4, 896, 896], P('row', 'col')
- second_params_new: float32 [8, 896, 896], P('col', 'row')
- second_moment_new: float32 [8, 896, 896], P('col', 'row')
All inputs are finite; a program needn't handle non-finite values.
Results may differ from a plain program's by a relative error of at most 0.022.
Values may be sent and summed in bfloat16 or wider, within the bound.
No kernel may reach another device: no remote copies, remote signals or barrier semaphores. Data moves between devices by JAX's collectives and lax.ppermute only.
A program may use at most 64 MiB of HBM per device.

v0:
```python
import jax
import jax.numpy as jnp
from jax import lax
from jax.sharding import PartitionSpec as P

outer_momentum = 0.9
outer_rate = 0.7


def passed_along(x, axis, by):
    length = lax.axis_size(axis)
    return lax.ppermute(x, axis, [(i, (i + by) % length) for i in range(length)])


def gelu_tanh(value):
    return jax.nn.gelu(value, approximate=True)


def nesterov(params, moment, grad):
    moment_new = outer_momentum * moment + grad
    return (params - outer_rate * (grad + outer_momentum * moment_new), moment_new)


def per_device(hidden_in, targets, first_params, first_moment, second_params, second_moment):
    inputs = hidden_in[0, 0]
    wanted = targets[0, 0]
    tokens = inputs.shape[0]
    offset = lax.axis_size("col") // 4
    pre = jnp.dot(
        inputs,
        lax.all_gather(first_params[0].astype(jnp.bfloat16), "col", axis=0, tiled=True),
        preferred_element_type=jnp.float32,
    )
    second_full = lax.all_gather(second_params[0].astype(jnp.bfloat16), "row", axis=0, tiled=True)
    active, slope = jax.vjp(gelu_tanh, pre)
    active_b = active.astype(jnp.bfloat16)
    output = jnp.dot(active_b, second_full, preferred_element_type=jnp.float32)
    error = ((output - wanted.astype(jnp.float32)) / tokens).astype(jnp.bfloat16)
    back = lax.dot_general(
        error, second_full, (((1,), (1,)), ((), ())), preferred_element_type=jnp.float32
    )
    grad_pre = slope(back)[0].astype(jnp.bfloat16)
    picked = active_b
    second_grad = lax.psum_scatter(
        lax.dot_general(
            picked, error, (((0,), (0,)), ((), ())), preferred_element_type=jnp.float32
        ).astype(jnp.bfloat16),
        "row",
        scatter_dimension=0,
        tiled=True,
    ).astype(jnp.float32) / lax.axis_size("row")
    picked = inputs
    first_grad = lax.psum_scatter(
        lax.dot_general(
            picked, grad_pre, (((0,), (0,)), ((), ())), preferred_element_type=jnp.float32
        ).astype(jnp.bfloat16),
        "col",
        scatter_dimension=0,
        tiled=True,
    ).astype(jnp.float32) / lax.axis_size("col")
    first_params_new, first_moment_new = nesterov(first_params, first_moment, first_grad[None])
    second_upd, second_mom = nesterov(second_params, second_moment, second_grad[None])
    stacked = jnp.stack([second_upd, second_mom])
    moved = passed_along(stacked.astype(jnp.bfloat16), "col", offset).astype(stacked.dtype)
    return (first_params_new, first_moment_new, moved[0], moved[1])


def solution(mesh):
    return jax.shard_map(
        per_device,
        mesh=mesh,
        in_specs=(
            P("row", "col", None, None),
            P("row", "col", None, None),
            P("row", "col", None),
            P("row", "col", None),
            P("col", "row", None),
            P("col", "row", None),
        ),
        out_specs=(
            P("row", "col", None),
            P("row", "col", None),
            P("col", "row", None),
            P("col", "row", None),
        ),
        check_vma=False,
    )
```

profile of v0, /device:TPU:0, one launch (start us, length us, event | category | flops | bytes accessed | tf_op | source)
XLA Modules:
  0.0 197.8 jit_solution(2901205608396926962)
XLA Ops:
  7.2 0.0 copy-start
  7.2 0.0 all-gather.5.cloned.1.call-start
  7.2 1.8 convert_element_type.54
  9.0 0.0 all-gather.5.cloned.1.call-update
  9.0 0.0 all-gather.7.cloned.1.call-start
  9.1 1.9 convert_element_type.57
  11.0 0.0 all-gather.7.cloned.1.call-update
  11.0 0.0 copy-start.5
  11.0 0.0 reduce-scatter.5.cloned.1.call-start
  11.1 47.0 %all-gather.5.cloned.1.call-done = bf16[1,896,896]{2,1,0:T(8,128)(2,1)} async-done(((bf16[1,112,896]{2,1,0:T(8,128)(2,1)}), bf16[1,896,896]{2,1,0:T(8,128)(2,1)}) %all-gather.5.cloned.1.call-update) | async-done | bytes 1605648 | tf_op jit(solution)/shard_map/all_gather | solution.py:31
  58.0 0.0 copy-done
  58.0 3.9 %fusion.13 = f32[512,896]{1,0:T(8,128)} fusion(bf16[1,896,896]{2,1,0:T(8,128)(2,1)} %all-gather.5.cloned.1.call-done, bf16[1,1,512,896]{3,2,1,0:T(8,128)(2,1)S(1)} %copy-done), kind=kOutput, calls=%fused_computation.19 | convolution fusion | flops 822083584 | bytes 4358144 | tf_op jit(solution)/shard_map/dot_general | solution.py:29
  61.9 16.5 %all-gather.7.cloned.1.call-done = bf16[1,896,896]{2,1,0:T(8,128)(2,1)} async-done(((bf16[1,224,896]{2,1,0:T(8,128)(2,1)}), bf16[1,896,896]{2,1,0:T(8,128)(2,1)}) %all-gather.7.cloned.1.call-update) | async-done | bytes 1605648 | tf_op jit(solution)/shard_map/all_gather | solution.py:34
  78.4 0.0 copy-done.5
  78.4 0.0 copy-start.6
  78.4 3.4 %fusion.8 = bf16[512,896]{1,0:T(8,128)(2,1)S(1)} fusion(bf16[1,896,896]{2,1,0:T(8,128)(2,1)} %all-gather.7.cloned.1.call-done, bf16[1,1,512,896]{3,2,1,0:T(8,128)(2,1)S(1)} %copy-done.5, f32[512,896]{1,0:T(8,128)} %fusion.13), kind=kOutput, calls=%fused_computation.11 | convolution fusion | flops 828047360 | bytes 5275648 | tf_op jit(solution)/shard_map/dot_general | solution.py:37
  81.8 0.0 copy-start.7
  81.8 1.0 copy-done.7
  82.8 0.0 copy-done.6
  82.8 2.4 %convolution_convert_fusion = bf16[896,896]{1,0:T(8,128)(2,1)} fusion(bf16[512,896]{1,0:T(8,128)(2,1)S(1)} %fusion.8, f32[512,896]{1,0:T(8,128)S(1)} %copy-done.6), kind=kOutput, calls=%fused_computation.13 | convolution fusion | flops 827015168 | bytes 4358144 | tf_op jit(solution)/shard_map/dot_general | solution.py:45
  85.2 0.0 reduce-scatter.5.cloned.1.call-update
  85.2 0.0 reduce-scatter.7.cloned.1.call-start
  85.2 4.9 %fusion.17 = bf16[896,896]{0,1:T(8,128)(2,1)S(1)} fusion(f32[512,896]{1,0:T(8,128)} %fusion.13, bf16[512,896]{1,0:T(8,128)(2,1)} %copy-done.7, bf16[1,896,896]{2,1,0:T(8,128)(2,1)} %all-gather.7.cloned.1.call-done, bf16[1,1,512,896]{3,2,1,0:T(8,128)(2,1)S(1)} %copy-done), kind=kOutput, calls=%fused_computation.21 | convolution fusion | flops 1654145024 | bytes 6881280 | tf_op jit(solution)/shard_map/dot_general | solution.py:54
  90.1 0.0 copy-start.1
  90.1 2.3 %copy.18 = bf16[896,896]{1,0:T(8,128)(2,1)} copy(bf16[896,896]{0,1:T(8,128)(2,1)S(1)} %fusion.17) | data formatting | bytes 3211264
  92.5 0.0 copy-start.3
  92.5 0.0 reduce-scatter.7.cloned.1.call-update
  92.5 0.0 copy-start.2
  92.5 21.0 %reduce-scatter.5.cloned.1.call-done = bf16[224,896]{1,0:T(8,128)(2,1)} async-done(((bf16[896,896]{1,0:T(8,128)(2,1)}), bf16[224,896]{1,0:T(8,128)(2,1)}) %reduce-scatter.5.cloned.1.call-update) | async-done | bytes 401424 | tf_op jit(solution)/shard_map/reduce_scatter | solution.py:44
  113.5 0.0 copy-done.1
  113.5 0.0 copy-done.3
  113.5 1.2 fusion.37
  114.8 0.0 copy-start.4
  114.8 1.0 pad_maximum_fusion
  115.8 1.5 collective-permute-start
  117.3 0.0 copy-done.2
  117.3 0.2 copy.15
  117.5 0.0 copy-done.4
  117.5 0.2 copy.14
  117.7 67.9 %reduce-scatter.7.cloned.1.call-done = bf16[112,896]{1,0:T(8,128)(2,1)} async-done(((bf16[896,896]{1,0:T(8,128)(2,1)}), bf16[112,896]{1,0:T(8,128)(2,1)}) %reduce-scatter.7.cloned.1.call-update) | async-done | bytes 200720
  185.6 1.1 copy.19
  186.7 0.1 bitcast_add_fusion.3
  186.9 0.9 copy.16
  187.8 0.9 copy.17
  188.7 0.0 collective-permute-done
  188.7 1.2 convert_element_type.68
  190.0 1.3 slice_bitcast_fusion
Async XLA Ops:
  7.2 50.9 %copy-start = (bf16[1,1,512,896]{3,2,1,0:T(8,128)(2,1)S(1)}, bf16[1,1,512,896]{3,2,1,0:T(8,128)(2,1)}, u32[]{:S(2)}) copy-start(bf16[1,1,512,896]{3,2,1,0:T(8,128)(2,1)} %param.6) | copy-start | bytes 2752516
  7.2 50.9 %all-gather.5.cloned.1.call-start = ((), (), s32[]{:S(2)}) async-start(), calls=%async_computation.3 | async-start | bytes 1806336 | tf_op jit(solution)/shard_map/all_gather | solution.py:31
  9.0 69.4 %all-gather.7.cloned.1.call-start = ((), (), s32[]{:S(2)}) async-start(), calls=%async_computation.4 | async-start | bytes 2007040 | tf_op jit(solution)/shard_map/all_gather | solution.py:34
  11.0 67.4 %copy-start.5 = (bf16[1,1,512,896]{3,2,1,0:T(8,128)(2,1)S(1)}, bf16[1,1,512,896]{3,2,1,0:T(8,128)(2,1)}, u32[]{:S(2)}) copy-start(bf16[1,1,512,896]{3,2,1,0:T(8,128)(2,1)} %param.7) | copy-start | bytes 2752516
  11.0 102.5 %reduce-scatter.5.cloned.1.call-start = ((), (), s32[]{:S(2)}) async-start(), calls=%async_computation.2 | async-start | bytes 2007040 | tf_op jit(solution)/shard_map/reduce_scatter | solution.py:44
  78.4 4.4 %copy-start.6 = (f32[512,896]{1,0:T(8,128)S(1)}, f32[512,896]{1,0:T(8,128)}, u32[]{:S(2)}) copy-start(f32[512,896]{1,0:T(8,128)} %fusion.13) | copy-start | bytes 5505028
  81.8 1.0 copy-start.7
  85.2 100.4 %reduce-scatter.7.cloned.1.call-start = ((), (), s32[]{:S(2)}) async-start(), calls=%async_computation.5 | async-start | bytes 1806336
  90.1 23.4 %copy-start.1 = (f32[1,224,896]{2,1,0:T(8,128)S(1)}, f32[1,224,896]{2,1,0:T(8,128)}, u32[]{:S(2)}) copy-start(f32[1,224,896]{2,1,0:T(8,128)} %param.10) | copy-start | bytes 2408452
  92.5 21.1 %copy-start.3 = (f32[1,224,896]{2,1,0:T(8,128)S(1)}, f32[1,224,896]{2,1,0:T(8,128)}, u32[]{:S(2)}) copy-start(f32[1,224,896]{2,1,0:T(8,128)} %param.11) | copy-start | bytes 2408452
  92.5 24.8 %copy-start.2 = (f32[1,112,896]{2,1,0:T(8,128)S(1)}, f32[1,112,896]{2,1,0:T(8,128)}, u32[]{:S(2)}) copy-start(f32[1,112,896]{2,1,0:T(8,128)} %param.8) | copy-start | bytes 1204228
  114.8 2.7 %copy-start.4 = (f32[1,112,896]{2,1,0:T(8,128)S(1)}, f32[1,112,896]{2,1,0:T(8,128)}, u32[]{:S(2)}) copy-start(f32[1,112,896]{2,1,0:T(8,128)} %param.9) | copy-start | bytes 1204228
  115.8 73.0 %collective-permute-start = (bf16[2,1,224,896]{3,2,1,0:T(8,128)(2,1)}, bf16[2,1,224,896]{3,2,1,0:T(8,128)(2,1)}, u32[]{:S(2)}, u32[]{:S(2)}) collective-permute-start(bf16[2,1,224,896]{3,2,1,0:T(8,128)(2,1)} %pad_maximum_fusion), channel_id=1, source_target_pairs={{0,2},{1,3},{2,4},{3,5},{4,6},{5,7},{6,0},{7,1},{8,10},{9,11},{10,... | collective-permute-start | bytes 2408456 | tf_op jit(solution)/shard_map/ppermute | solution.py:12
Sparse Core Ops, SparseCore 0:
  10.7 47.2 all-gather.4
  60.2 18.1 all-gather.6
  85.3 28.1 reduce-scatter.4
  116.9 68.7 reduce-scatter.6
where the time goes:
time: 198 us
  waiting for transfers between devices  152 us (77%)
  matrix products  14.6 us (7%)
  between operations  13.9 us (7%)
  local copies, waits for them, and re-layouts  7.96 us (4%)
  other arithmetic  7.29 us (4%)
    unnamed x5, waiting for transfers between devices  68 us
    all_gather x1, waiting for transfers between devices, per_device(): lax.all_gather(first_params[0].astype(jnp.bfloat16), 'col', axis=0, tiled...  47 us
    reduce_scatter x1, waiting for transfers between devices, per_device(): lax.psum_scatter(lax.dot_general(picked, error, (((0,), (0,)), ((), ())),...  21 us
    all_gather x1, waiting for transfers between devices, per_device(): lax.all_gather(second_params[0].astype(jnp.bfloat16), 'row', axis=0, tile...  16.5 us
    unnamed x22, local copies, waits for them, and re-layouts  6.71 us
    dot_general x1, matrix products, per_device(): lax.dot_general(picked, grad_pre, (((0,), (0,)), ((), ())), preferred_ele...  4.88 us
  transfers between devices with their start and end apart: 5, of which 4 were waited for; matrix products, arithmetic and copies ran while one was open for 9% of the time, Pallas kernels for 0%

commit v1 on v0

--- a/solution.py
+++ b/solution.py
@@ -5,6 +5,13 @@
 
 outer_momentum = 0.9
 outer_rate = 0.7
+
+
+def gather_over(x, name, dim):
+    n_dev = lax.axis_size(name)
+    blocks = jnp.stack([x for _ in range(n_dev)])
+    blocks = lax.all_to_all(blocks, name, split_axis=0, concat_axis=0)
+    return jnp.concatenate(blocks, axis=dim)
 
 
 def passed_along(x, axis, by):
@@ -28,7 +35,7 @@
     offset = lax.axis_size("col") // 4
     pre = jnp.dot(
         inputs,
-        lax.all_gather(first_params[0].astype(jnp.bfloat16), "col", axis=0, tiled=True),
+        gather_over(first_params[0].astype(jnp.bfloat16), "col", 0),
         preferred_element_type=jnp.float32,
     )
     second_full = lax.all_gather(second_params[0].astype(jnp.bfloat16), "row", axis=0, tiled=True)

time: 198 us -> 176 us (0.89)
  waiting for transfers between devices: 152 us -> 125 us
  starting transfers between devices: 1.66 us -> 9.06 us
    all_gather x1 -> x0, waiting for transfers between devices: 47 us -> none  [per_device(): lax.all_gather(first_params[0].astype(jnp.bfloat16), 'col', axis=0, tiled...]
    all_to_all x0 -> x1, waiting for transfers between devices: none -> 36.8 us  [gather_over(): blocks = lax.all_to_all(blocks, name, split_axis=0, concat_axis=0)]
    all_gather x1, waiting for transfers between devices: 16.5 us -> 0.01 us  [per_device(): lax.all_gather(second_params[0].astype(jnp.bfloat16), 'row', axis=0, tile...]
    all_to_all x0 -> x1, starting transfers between devices: none -> 7.44 us  [gather_over(): blocks = lax.all_to_all(blocks, name, split_axis=0, concat_axis=0)]
    unnamed x5 -> x4, waiting for transfers between devices: 68 us -> 68.1 us
    unnamed x22 -> x20, local copies, waits for them, and re-layouts: 6.71 us -> 6.69 us
  transfers between devices with their start and end apart: 5 -> 5, of which waited for: 4 -> 3; matrix products, arithmetic and copies ran while one was open for 9% -> 9% of each run, Pallas kernels for 0% -> 0%
where the time goes in v1:
time: 176 us
  waiting for transfers between devices  125 us (71%)
  between operations  13.9 us (8%)
  matrix products  13.4 us (8%)
  local copies, waits for them, and re-layouts  9.24 us (5%)
  starting transfers between devices  9.06 us (5%)
  other arithmetic  5.48 us (3%)
    unnamed x4, waiting for transfers between devices  68.1 us
    all_to_all x1, waiting for transfers between devices, gather_over(): blocks = lax.all_to_all(blocks, name, split_axis=0, concat_axis=0)  36.8 us
    reduce_scatter x1, waiting for transfers between devices, per_device(): lax.psum_scatter(lax.dot_general(picked, error, (((0,), (0,)), ((), ())),...  20.2 us
    all_to_all x1, starting transfers between devices, gather_over(): blocks = lax.all_to_all(blocks, name, split_axis=0, concat_axis=0)  7.44 us
    unnamed x20, local copies, waits for them, and re-layouts  6.69 us
    dot_general x1, matrix products, per_device(): lax.dot_general(picked, grad_pre, (((0,), (0,)), ((), ())), preferred_ele...  4.88 us
    dot_general x1, matrix products, per_device(): output = jnp.dot(active_b, second_full, preferred_element_type=jnp.float32)  3.64 us
  transfers between devices with their start and end apart: 5, of which 3 were waited for; matrix products, arithmetic and copies ran while one was open for 9% of the time, Pallas kernels for 0%

profile of v1, /device:TPU:0, one launch (start us, length us, event | category | flops | bytes accessed | tf_op | source)
XLA Modules:
  0.0 176.1 jit_solution(2760551912253480810)
XLA Ops:
  7.2 0.0 copy-start
  7.2 1.1 convert_bitcast_fusion
  8.3 1.3 stack.11
  9.6 0.0 copy-start.1
  9.6 7.4 %all-to-all-start = ((bf16[8,112,896]{2,1,0:T(8,128)(2,1)}), bf16[8,112,896]{2,1,0:T(8,128)(2,1)S(1)}, u32[]{:S(2)}, u32[]{:S(2)}) async-start(bf16[8,112,896]{2,1,0:T(8,128)(2,1)} %stack.11), calls=%async_computation | async-start | bytes 3211264 | tf_op jit(solution)/shard_map/all_to_all | solution.py:13
  17.0 0.0 all-gather.3.cloned.1.call-start
  17.1 0.0 copy-done.1
  17.1 0.8 convert_element_type.54
  17.9 0.0 all-gather.3.cloned.1.call-update
  17.9 0.0 reduce-scatter.5.cloned.1.call-start
  17.9 36.8 %all-to-all-done = bf16[8,112,896]{2,1,0:T(8,128)(2,1)S(1)} async-done(((bf16[8,112,896]{2,1,0:T(8,128)(2,1)}), bf16[8,112,896]{2,1,0:T(8,128)(2,1)S(1)}, u32[]{:S(2)}, u32[]{:S(2)}) %all-to-all-start) | async-done | bytes 1605664 | tf_op jit(solution)/shard_map/all_to_all | solution.py:13
  54.7 0.0 copy-done
  54.7 2.5 %fusion.21 = f32[512,896]{1,0:T(8,128)} fusion(bf16[896,896]{1,0:T(8,128)(2,1)S(1)} %bitcast.62, bf16[1,1,512,896]{3,2,1,0:T(8,128)(2,1)S(1)} %copy-done), kind=kOutput, calls=%fused_computation.21 | convolution fusion | flops 822083584 | bytes 4358144 | tf_op jit(solution)/shard_map/dot_general | solution.py:36
  57.2 0.0 copy-start.5
  57.2 0.0 all-gather.3.cloned.1.call-done
  57.2 3.6 %fusion.8 = bf16[512,896]{1,0:T(8,128)(2,1)S(1)} fusion(bf16[1,896,896]{2,1,0:T(8,128)(2,1)} %all-gather.3.cloned.1.call-done, bf16[1,1,512,896]{3,2,1,0:T(8,128)(2,1)} %param.7, f32[512,896]{1,0:T(8,128)} %fusion.21), kind=kOutput, calls=%fused_computation.11 | convolution fusion | flops 828047360 | bytes 5275648 | tf_op jit(solution)/shard_map/dot_general | solution.py:44
  60.9 0.0 copy-start.6
  60.9 1.0 copy-done.6
  61.8 0.0 copy-done.5
  61.8 2.4 %convolution_convert_fusion = bf16[896,896]{1,0:T(8,128)(2,1)} fusion(bf16[512,896]{1,0:T(8,128)(2,1)S(1)} %fusion.8, f32[512,896]{1,0:T(8,128)S(1)} %copy-done.5), kind=kOutput, calls=%fused_computation.13 | convolution fusion | flops 827015168 | bytes 4358144 | tf_op jit(solution)/shard_map/dot_general | solution.py:52
  64.2 0.0 reduce-scatter.5.cloned.1.call-update
  64.3 0.0 reduce-scatter.7.cloned.1.call-start
  64.3 4.9 %fusion.15 = bf16[896,896]{0,1:T(8,128)(2,1)S(1)} fusion(f32[512,896]{1,0:T(8,128)} %fusion.21, bf16[512,896]{1,0:T(8,128)(2,1)} %copy-done.6, bf16[1,896,896]{2,1,0:T(8,128)(2,1)} %all-gather.3.cloned.1.call-done, bf16[1,1,512,896]{3,2,1,0:T(8,128)(2,1)S(1)} %copy-done), kind=kOutput, calls=%fused_computation.19 | convolution fusion | flops 1654145024 | bytes 6881280 | tf_op jit(solution)/shard_map/dot_general | solution.py:61
  69.2 2.3 %copy.18 = bf16[896,896]{1,0:T(8,128)(2,1)} copy(bf16[896,896]{0,1:T(8,128)(2,1)S(1)} %fusion.15) | data formatting | bytes 3211264
  71.5 0.0 copy-start.3
  71.5 0.0 reduce-scatter.7.cloned.1.call-update
  71.6 0.0 copy-start.2
  71.6 20.2 %reduce-scatter.5.cloned.1.call-done = bf16[224,896]{1,0:T(8,128)(2,1)} async-done(((bf16[896,896]{1,0:T(8,128)(2,1)}), bf16[224,896]{1,0:T(8,128)(2,1)}) %reduce-scatter.5.cloned.1.call-update) | async-done | bytes 401424 | tf_op jit(solution)/shard_map/reduce_scatter | solution.py:51
  91.7 0.0 copy-done.3
  91.7 1.2 fusion.36
  93.0 0.0 copy-start.4
  93.0 1.0 pad_maximum_fusion
  94.0 1.5 collective-permute-start
  95.5 0.0 copy-done.2
  95.5 0.2 copy.15
  95.7 0.0 copy-done.4
  95.7 0.2 copy.14
  95.9 68.1 %reduce-scatter.7.cloned.1.call-done = bf16[112,896]{1,0:T(8,128)(2,1)} async-done(((bf16[896,896]{1,0:T(8,128)(2,1)}), bf16[112,896]{1,0:T(8,128)(2,1)}) %reduce-scatter.7.cloned.1.call-update) | async-done | bytes 200720
  164.0 1.1 copy.19
  165.1 0.1 bitcast_add_fusion.3
  165.2 0.9 copy.16
  166.1 0.9 copy.17
  167.1 0.0 collective-permute-done
  167.1 1.2 convert_element_type.65
  168.3 1.3 slice_bitcast_fusion
Async XLA Ops:
  7.2 47.6 %copy-start = (bf16[1,1,512,896]{3,2,1,0:T(8,128)(2,1)S(1)}, bf16[1,1,512,896]{3,2,1,0:T(8,128)(2,1)}, u32[]{:S(2)}) copy-start(bf16[1,1,512,896]{3,2,1,0:T(8,128)(2,1)} %param.6) | copy-start | bytes 2752516
  9.6 7.5 %copy-start.1 = (f32[1,224,896]{2,1,0:T(8,128)S(1)}, f32[1,224,896]{2,1,0:T(8,128)}, u32[]{:S(2)}) copy-start(f32[1,224,896]{2,1,0:T(8,128)} %param.10) | copy-start | bytes 2408452
  9.6 45.1 %all-to-all-start = ((bf16[8,112,896]{2,1,0:T(8,128)(2,1)}), bf16[8,112,896]{2,1,0:T(8,128)(2,1)S(1)}, u32[]{:S(2)}, u32[]{:S(2)}) async-start(bf16[8,112,896]{2,1,0:T(8,128)(2,1)} %stack.11), calls=%async_computation | async-start | bytes 3211264 | tf_op jit(solution)/shard_map/all_to_all | solution.py:13
  17.0 40.2 %all-gather.3.cloned.1.call-start = ((), (), s32[]{:S(2)}) async-start(), calls=%async_computation.4 | async-start | bytes 2007040 | tf_op jit(solution)/shard_map/all_gather | solution.py:41
  17.9 73.8 %reduce-scatter.5.cloned.1.call-start = ((), (), s32[]{:S(2)}) async-start(), calls=%async_computation.3 | async-start | bytes 2007040 | tf_op jit(solution)/shard_map/reduce_scatter | solution.py:51
  57.2 4.6 %copy-start.5 = (f32[512,896]{1,0:T(8,128)S(1)}, f32[512,896]{1,0:T(8,128)}, u32[]{:S(2)}) copy-start(f32[512,896]{1,0:T(8,128)} %fusion.21) | copy-start | bytes 5505028
  60.9 1.0 copy-start.6
  64.3 99.7 %reduce-scatter.7.cloned.1.call-start = ((), (), s32[]{:S(2)}) async-start(), calls=%async_computation.5 | async-start | bytes 1806336
  71.5 20.2 %copy-start.3 = (f32[1,224,896]{2,1,0:T(8,128)S(1)}, f32[1,224,896]{2,1,0:T(8,128)}, u32[]{:S(2)}) copy-start(f32[1,224,896]{2,1,0:T(8,128)} %param.11) | copy-start | bytes 2408452
  71.6 23.9 %copy-start.2 = (f32[1,112,896]{2,1,0:T(8,128)S(1)}, f32[1,112,896]{2,1,0:T(8,128)}, u32[]{:S(2)}) copy-start(f32[1,112,896]{2,1,0:T(8,128)} %param.8) | copy-start | bytes 1204228
  93.0 2.7 %copy-start.4 = (f32[1,112,896]{2,1,0:T(8,128)S(1)}, f32[1,112,896]{2,1,0:T(8,128)}, u32[]{:S(2)}) copy-start(f32[1,112,896]{2,1,0:T(8,128)} %param.9) | copy-start | bytes 1204228
  94.0 73.1 %collective-permute-start = (bf16[2,1,224,896]{3,2,1,0:T(8,128)(2,1)}, bf16[2,1,224,896]{3,2,1,0:T(8,128)(2,1)}, u32[]{:S(2)}, u32[]{:S(2)}) collective-permute-start(bf16[2,1,224,896]{3,2,1,0:T(8,128)(2,1)} %pad_maximum_fusion), channel_id=1, source_target_pairs={{0,2},{1,3},{2,4},{3,5},{4,6},{5,7},{6,0},{7,1},{8,10},{9,11},{10,... | collective-permute-start | bytes 2408456 | tf_op jit(solution)/shard_map/ppermute | solution.py:19
Sparse Core Ops, SparseCore 0:
  20.0 21.2 all-gather.2
  64.4 27.2 reduce-scatter.4
  95.2 68.7 reduce-scatter.6
